TPU v7x, 256 devices: a whole 4x4x8 slice. The times are simulated.
256 devices in a mesh: seq: 16 (over y_hi, x, core), dp: 16 (over y_lo, z).
Axes of the slice: x: 4, y: 4 (y_hi: 2, y_lo: 2; y = y_hi * 2 + y_lo), z: 8, core: 2. Of those that a mesh axis runs over, the one named last changes fastest.
Arguments:
- query: bfloat16 [16, 3072, 1280], P('dp', 'seq'), may hold values from -52 to 52, as said below
- keys: bfloat16 [16, 3072, 1280], P('dp', 'seq'), may hold values from -6 to 6, as said below
- values: bfloat16 [16, 3072, 1280], P('dp', 'seq'), may hold values from -6 to 6
- attn: bfloat16 [16, 3072, 1280], P('dp', 'seq'), may hold values from -6 to 6
- d_block: bfloat16 [16, 3072, 1280], P('dp', 'seq'), may hold values from -6 to 6
- w_out: bfloat16 [1280, 1280], P('dp'), may hold values from -0.15625 to 0.15625
Outputs:
- d_query: bfloat16 [16, 3072, 1280], P('dp', 'seq')
- d_keys: bfloat16 [16, 3072, 1280], P('dp', 'seq')
- d_values: bfloat16 [16, 3072, 1280], P('dp', 'seq')
- d_weight: float32 [1280, 1280], P('dp')
Inputs may be any that keep to these rules, and one draw needn't show every extreme that they name: Some query patches may lie along the sum of two keys of the same video. keys has entries of order one.
All inputs are finite; a program needn't handle non-finite values.
Results may differ from a plain program's by a relative error of at most 0.0058.
Values may be sent and summed in bfloat16 or wider, within the bound.
No kernel may reach another device: no remote copies, remote signals or barrier semaphores. Data moves between devices by JAX's collectives and lax.ppermute only.
A program may use at most 64 MiB of HBM per device.

v0:
```python
import jax
import jax.numpy as jnp
from jax import lax
from jax.sharding import Mesh
from jax.sharding import PartitionSpec as P

HEAD_DIM = 80
DP = ("dp_0", "dp_1")


def reduced_to_own(blocks, axes, order):
    lengths = [lax.axis_size(a) for a in axes]
    blocks = blocks.reshape(*lengths, *blocks.shape[1:])
    blocks = blocks.transpose(*order, *range(len(axes), blocks.ndim))
    blocks = blocks.reshape(-1, *blocks.shape[len(axes) :])
    for k in order:
        blocks = lax.psum_scatter(blocks, axes[k], scatter_dimension=0, tiled=True)
    return blocks[0]


def split_up(x, dim, size):
    before, after = (x.shape[:dim], x.shape[dim + 1 :])
    return jnp.moveaxis(x.reshape(*before, size, -1, *after), dim, 0)


def scatter_axes(x, axes, order, dim):
    size = lax.axis_size(axes)
    return reduced_to_own(split_up(x, dim, size), axes, order)


def over_pieces(x, axis):
    blocks = lax.all_gather(x, axis)
    return blocks.sum(axis=0)


def head_backward(query_h, keys_h, values_h, dout_h, delta_h):
    patch_total = query_h.shape[0]
    block_rows = min(512, patch_total)
    while patch_total % block_rows != 0:
        block_rows = block_rows // 2
    block_total = patch_total // block_rows
    score_scale = HEAD_DIM ** (-0.5)
    contract_last = (((1,), (1,)), ((), ()))
    contract_first = (((0,), (0,)), ((), ()))

    def one_block(carry, inputs):
        keys_grad, values_grad = carry
        query_block, dout_block, delta_block = inputs
        scores = (
            lax.dot_general(query_block, keys_h, contract_last, preferred_element_type=jnp.float32)
            * score_scale
        )
        row_max = jnp.max(scores, axis=1, keepdims=True)
        lse = row_max + jnp.log(jnp.sum(jnp.exp(scores - row_max), axis=1, keepdims=True))
        probs = jnp.exp(scores - lse)
        probs_low = probs.astype(jnp.bfloat16)
        values_grad = values_grad + lax.dot_general(
            probs_low, dout_block, contract_first, preferred_element_type=jnp.float32
        )
        d_probs = lax.dot_general(
            dout_block, values_h, contract_last, preferred_element_type=jnp.float32
        )
        d_scores = (score_scale * probs * (d_probs - delta_block[:, None])).astype(jnp.bfloat16)
        query_grad = jnp.dot(d_scores, keys_h, preferred_element_type=jnp.float32)
        keys_grad = keys_grad + lax.dot_general(
            d_scores, query_block, contract_first, preferred_element_type=jnp.float32
        )
        return ((keys_grad, values_grad), query_grad.astype(jnp.bfloat16))

    empty = jnp.zeros((patch_total, HEAD_DIM), jnp.float32)
    blocked = (
        query_h.reshape(block_total, block_rows, HEAD_DIM),
        dout_h.reshape(block_total, block_rows, HEAD_DIM),
        delta_h.reshape(block_total, block_rows),
    )
    (keys_grad, values_grad), query_blocks = lax.scan(one_block, (empty, empty), blocked)
    return (
        query_blocks.reshape(patch_total, HEAD_DIM),
        keys_grad.astype(jnp.bfloat16),
        values_grad.astype(jnp.bfloat16),
    )


def body(query, keys, values, attn, d_block, w_out):
    seq_count = lax.axis_size("seq")
    dp_count = lax.axis_size(DP)
    tok_rows = query.shape[1]
    features = query.shape[2]
    head_here = features // HEAD_DIM // seq_count
    grad_y = d_block.reshape(tok_rows, features)
    attn_rows = attn.reshape(tok_rows, features)
    d_out = lax.dot_general(
        grad_y,
        lax.all_gather(w_out, DP, axis=0, tiled=True),
        (((1,), (1,)), ((), ())),
        preferred_element_type=jnp.float32,
    ).astype(jnp.bfloat16)

    def split_heads(array):
        return array.reshape(tok_rows, seq_count, head_here, HEAD_DIM)

    row_local = jnp.sum(
        split_heads(d_out).astype(jnp.float32) * split_heads(attn_rows).astype(jnp.float32), axis=3
    )
    row_terms = lax.all_to_all(row_local, "seq", split_axis=1, concat_axis=0, tiled=True)
    query_all, keys_all, values_all, dout_all = (
        lax.all_to_all(split_heads(query), "seq", split_axis=1, concat_axis=0, tiled=True),
        lax.all_to_all(split_heads(keys), "seq", split_axis=1, concat_axis=0, tiled=True),
        lax.all_to_all(split_heads(values), "seq", split_axis=1, concat_axis=0, tiled=True),
        lax.all_to_all(split_heads(d_out), "seq", split_axis=1, concat_axis=0, tiled=True),
    )
    gradient = head_backward(
        query_all[:, 0, 0],
        keys_all[:, 0, 0],
        values_all[:, 0, 0],
        dout_all[:, 0, 0],
        row_terms[:, 0, 0],
    )
    query_list = [gradient[0]]
    keys_list = [gradient[1]]
    values_list = [gradient[2]]
    query_heads = jnp.stack(query_list, axis=1)[:, None]
    keys_heads = jnp.stack(keys_list, axis=1)[:, None]
    values_heads = jnp.stack(values_list, axis=1)[:, None]
    query_back, keys_back, values_back = (
        lax.all_to_all(query_heads, "seq", split_axis=0, concat_axis=1, tiled=True),
        lax.all_to_all(keys_heads, "seq", split_axis=0, concat_axis=1, tiled=True),
        lax.all_to_all(values_heads, "seq", split_axis=0, concat_axis=1, tiled=True),
    )
    factor = 1.0 / float(dp_count * tok_rows * seq_count) ** 0.5
    contract_first = (((0,), (0,)), ((), ()))
    partial_rows = scatter_axes(
        lax.dot_general(attn_rows, grad_y, contract_first, preferred_element_type=jnp.float32)
        * factor,
        DP,
        (1, 0),
        0,
    )
    d_weight = over_pieces(partial_rows, "seq")
    shape_out = (1, tok_rows, features)
    return (
        query_back.reshape(shape_out),
        keys_back.reshape(shape_out),
        values_back.reshape(shape_out),
        d_weight,
    )


def solution(mesh):
    finer = Mesh(mesh.devices.reshape(mesh.shape["seq"], 2, 8), ("seq", "dp_0", "dp_1"))
    in_specs = (
        P(DP, "seq", None),
        P(DP, "seq", None),
        P(DP, "seq", None),
        P(DP, "seq", None),
        P(DP, "seq", None),
        P(DP, None),
    )
    out_specs = (P(DP, "seq", None), P(DP, "seq", None), P(DP, "seq", None), P(DP, None))
    return jax.shard_map(body, mesh=finer, in_specs=in_specs, out_specs=out_specs, check_vma=False)
```

profile of v0, /device:TPU:1, one launch (start us, length us, event | category | flops | bytes accessed | tf_op | source)
XLA Modules:
  0.0 369.2 jit_solution(4399982114246284704)
XLA Ops:
  9.0 2.1 convolution_multiply_fusion
  11.1 3.2 copy.106
  16.5 8.4 %all-to-all-start.3 = ((bf16[192,16,1,80]{0,3,2,1:T(8,128)(2,1)}), bf16[192,16,1,80]{0,3,2,1:T(8,128)(2,1)S(1)}, u32[]{:S(2)}, u32[]{:S(2)}) async-start(bf16[192,16,1,80]{0,3,2,1:T(8,128)(2,1)} %bitcast.17), calls=%async_computation.3 | async-start | bytes 1310720 | tf_op jit(solution)/shard_map/all_to_all | solution.py:109
  25.0 84.7 %reduce-scatter.3.cloned.1.call-done = f32[2,80,1280]{2,1,0:T(8,128)} async-done(((f32[16,80,1280]{2,1,0:T(8,128)}), f32[2,80,1280]{2,1,0:T(8,128)}) %reduce-scatter.3.cloned.1.call-update) | async-done | bytes 819216 | tf_op jit(solution)/shard_map/reduce_scatter | solution.py:17
  110.8 7.6 %all-to-all-start = ((bf16[192,16,1,80]{0,3,2,1:T(8,128)(2,1)}), bf16[192,16,1,80]{0,3,2,1:T(8,128)(2,1)S(1)}, u32[]{:S(2)}, u32[]{:S(2)}) async-start(bf16[192,16,1,80]{0,3,2,1:T(8,128)(2,1)} %bitcast.1), calls=%async_computation | async-start | bytes 1310720 | tf_op jit(solution)/shard_map/all_to_all | solution.py:107
  120.6 18.7 %all-to-all-done = bf16[192,16,1,80]{0,3,2,1:T(8,128)(2,1)S(1)} async-done(((bf16[192,16,1,80]{0,3,2,1:T(8,128)(2,1)}), bf16[192,16,1,80]{0,3,2,1:T(8,128)(2,1)S(1)}, u32[]{:S(2)}, u32[]{:S(2)}) %all-to-all-start) | async-done | bytes 491552 | tf_op jit(solution)/shard_map/all_to_all | solution.py:107
  139.3 4.8 %all-to-all-start.1 = ((bf16[192,16,1,80]{0,3,2,1:T(8,128)(2,1)}), bf16[192,16,1,80]{0,3,2,1:T(8,128)(2,1)S(1)}, u32[]{:S(2)}, u32[]{:S(2)}) async-start(bf16[192,16,1,80]{0,3,2,1:T(8,128)(2,1)} %bitcast.124), calls=%async_computation.1 | async-start | bytes 1310720 | tf_op jit(solution)/shard_map/all_to_all | solution.py:108
  144.1 3.2 convolution_convert_fusion.1
  149.9 7.1 %all-to-all-done.1 = bf16[192,16,1,80]{0,3,2,1:T(8,128)(2,1)S(1)} async-done(((bf16[192,16,1,80]{0,3,2,1:T(8,128)(2,1)}), bf16[192,16,1,80]{0,3,2,1:T(8,128)(2,1)S(1)}, u32[]{:S(2)}, u32[]{:S(2)}) %all-to-all-start.1) | async-done | bytes 491552 | tf_op jit(solution)/shard_map/all_to_all | solution.py:108
  157.0 11.4 %all_to_all.120 = f32[192,16,1]{0,2,1:T(1,128)S(1)} all-to-all(f32[192,16,1]{0,2,1:T(1,128)S(1)} %reduce_sum.30), channel_id=1, replica_groups=mesh['seq'=16,'dp_0'=2,'dp_1'=8] {'seq'}, dimensions={1} | all-to-all | bytes 24576 | tf_op jit(solution)/shard_map/all_to_all | solution.py:105
  168.4 4.4 %all-to-all-start.2 = ((bf16[192,16,1,80]{0,3,2,1:T(8,128)(2,1)}), bf16[192,16,1,80]{0,3,2,1:T(8,128)(2,1)}, u32[]{:S(2)}, u32[]{:S(2)}) async-start(bf16[192,16,1,80]{0,3,2,1:T(8,128)(2,1)} %bitcast.12), calls=%async_computation.2 | async-start | bytes 1310720 | tf_op jit(solution)/shard_map/all_to_all | solution.py:110
  174.3 2.3 copy.110
  178.3 7.7 %all-to-all-done.2 = bf16[192,16,1,80]{0,3,2,1:T(8,128)(2,1)} async-done(((bf16[192,16,1,80]{0,3,2,1:T(8,128)(2,1)}), bf16[192,16,1,80]{0,3,2,1:T(8,128)(2,1)}, u32[]{:S(2)}, u32[]{:S(2)}) %all-to-all-start.2) | async-done | bytes 491552 | tf_op jit(solution)/shard_map/all_to_all | solution.py:110
  186.0 2.3 copy.112
  188.3 101.8 %while.15 = (s32[]{:T(128)}, f32[3072,80]{0,1:T(8,128)S(1)}, f32[3072,80]{0,1:T(8,128)S(1)}, bf16[6,512,80]{1,2,0:T(8,128)(2,1)}, bf16[6,512,80]{2,1,0:T(8,128)(...) while((s32[]{:T(128)}, f32[3072,80]{0,1:T(8,128)S(1)}, ...), condition=%wide.region_4.5_spmd.clone, body=%wide.region_1.4_spmd.clone.sunk | while | flops 1281334784 | bytes 91267760 | solution.py:76
  188.3 2.0 multiply_reduce_fusion.2
  190.3 2.6 copy-done.2
  194.1 4.5 %convolution_add_fusion.5 = f32[3072,80]{0,1:T(8,128)S(1)} fusion(f32[512,3072]{1,0:T(8,128)} %copy-done.2, f32[512]{0:T(512)S(1)} %log_add_fusion.2, f32[3072,80]{0,1:T(8,128)S(1)} %get-tuple-element.223, pred[]{:T(512)S(6)} %compare.3, bf16[6,512,80]{2,1,0:T(8,128)(2,1)} %get-tuple-element.238, s32[]{:T(128)} %get-tuple-element.221), kind=kOutput, calls=%fused_computation.5.clone.1 | convolution fusion | flops 256868352 | bytes 8391169 | tf_op jit(solution)/shard_map/while/body/eval_jaxpr/dot_general | solution.py:57
  198.9 3.0 multiply_convert_fusion.2
  205.4 2.0 multiply_reduce_fusion.2
  207.4 2.6 copy-done.2
  211.1 4.3 %convolution_add_fusion.5 = f32[3072,80]{0,1:T(8,128)S(1)} fusion(f32[512,3072]{1,0:T(8,128)} %copy-done.2, f32[512]{0:T(512)S(1)} %log_add_fusion.2, f32[3072,80]{0,1:T(8,128)S(1)} %get-tuple-element.223, pred[]{:T(512)S(6)} %compare.3, bf16[6,512,80]{2,1,0:T(8,128)(2,1)} %get-tuple-element.238, s32[]{:T(128)} %get-tuple-element.221), kind=kOutput, calls=%fused_computation.5.clone.1 | convolution fusion | flops 256868352 | bytes 8391169 | tf_op jit(solution)/shard_map/while/body/eval_jaxpr/dot_general | solution.py:57
  215.8 3.0 multiply_convert_fusion.2
  222.2 2.0 multiply_reduce_fusion.2
  224.2 2.6 copy-done.2
  228.0 4.4 %convolution_add_fusion.5 = f32[3072,80]{0,1:T(8,128)S(1)} fusion(f32[512,3072]{1,0:T(8,128)} %copy-done.2, f32[512]{0:T(512)S(1)} %log_add_fusion.2, f32[3072,80]{0,1:T(8,128)S(1)} %get-tuple-element.223, pred[]{:T(512)S(6)} %compare.3, bf16[6,512,80]{2,1,0:T(8,128)(2,1)} %get-tuple-element.238, s32[]{:T(128)} %get-tuple-element.221), kind=kOutput, calls=%fused_computation.5.clone.1 | convolution fusion | flops 256868352 | bytes 8391169 | tf_op jit(solution)/shard_map/while/body/eval_jaxpr/dot_general | solution.py:57
  232.7 3.0 multiply_convert_fusion.2
  239.2 2.0 multiply_reduce_fusion.2
  241.2 2.6 copy-done.2
  244.9 4.4 %convolution_add_fusion.5 = f32[3072,80]{0,1:T(8,128)S(1)} fusion(f32[512,3072]{1,0:T(8,128)} %copy-done.2, f32[512]{0:T(512)S(1)} %log_add_fusion.2, f32[3072,80]{0,1:T(8,128)S(1)} %get-tuple-element.223, pred[]{:T(512)S(6)} %compare.3, bf16[6,512,80]{2,1,0:T(8,128)(2,1)} %get-tuple-element.238, s32[]{:T(128)} %get-tuple-element.221), kind=kOutput, calls=%fused_computation.5.clone.1 | convolution fusion | flops 256868352 | bytes 8391169 | tf_op jit(solution)/shard_map/while/body/eval_jaxpr/dot_general | solution.py:57
  249.9 3.0 multiply_convert_fusion.2
  256.4 2.0 multiply_reduce_fusion.2
  258.3 2.6 copy-done.2
  262.1 4.3 %convolution_add_fusion.5 = f32[3072,80]{0,1:T(8,128)S(1)} fusion(f32[512,3072]{1,0:T(8,128)} %copy-done.2, f32[512]{0:T(512)S(1)} %log_add_fusion.2, f32[3072,80]{0,1:T(8,128)S(1)} %get-tuple-element.223, pred[]{:T(512)S(6)} %compare.3, bf16[6,512,80]{2,1,0:T(8,128)(2,1)} %get-tuple-element.238, s32[]{:T(128)} %get-tuple-element.221), kind=kOutput, calls=%fused_computation.5.clone.1 | convolution fusion | flops 256868352 | bytes 8391169 | tf_op jit(solution)/shard_map/while/body/eval_jaxpr/dot_general | solution.py:57
  266.8 3.0 multiply_convert_fusion.2
  273.2 2.0 multiply_reduce_fusion.2
  275.2 2.6 copy-done.2
  279.0 4.3 %convolution_add_fusion.5 = f32[3072,80]{0,1:T(8,128)S(1)} fusion(f32[512,3072]{1,0:T(8,128)} %copy-done.2, f32[512]{0:T(512)S(1)} %log_add_fusion.2, f32[3072,80]{0,1:T(8,128)S(1)} %get-tuple-element.223, pred[]{:T(512)S(6)} %compare.3, bf16[6,512,80]{2,1,0:T(8,128)(2,1)} %get-tuple-element.238, s32[]{:T(128)} %get-tuple-element.221), kind=kOutput, calls=%fused_computation.5.clone.1 | convolution fusion | flops 256868352 | bytes 8391169 | tf_op jit(solution)/shard_map/while/body/eval_jaxpr/dot_general | solution.py:57
  283.6 3.0 multiply_convert_fusion.2
  292.0 2.2 reshape.106
  294.3 4.1 %all-to-all-start.7 = ((bf16[16,2,7680]{2,1,0:T(2,128)(2,1)}), bf16[16,2,7680]{2,1,0:T(2,128)(2,1)S(1)}, u32[]{:S(2)}, u32[]{:S(2)}) async-start(bf16[16,2,7680]{2,1,0:T(2,128)(2,1)} %reshape.106), calls=%async_computation.7 | async-start | bytes 983040 | tf_op jit(solution)/shard_map/all_to_all | solution.py:128
  299.7 2.2 reshape.104
  301.9 7.6 %all-to-all-done.7 = bf16[16,2,7680]{2,1,0:T(2,128)(2,1)S(1)} async-done(((bf16[16,2,7680]{2,1,0:T(2,128)(2,1)}), bf16[16,2,7680]{2,1,0:T(2,128)(2,1)S(1)}, u32[]{:S(2)}, u32[]{:S(2)}) %all-to-all-start.7) | async-done | bytes 491552 | tf_op jit(solution)/shard_map/all_to_all | solution.py:128
  309.5 4.4 %all-to-all-start.6 = ((bf16[16,2,7680]{2,1,0:T(2,128)(2,1)}), bf16[16,2,7680]{2,1,0:T(2,128)(2,1)S(1)}, u32[]{:S(2)}, u32[]{:S(2)}) async-start(bf16[16,2,7680]{2,1,0:T(2,128)(2,1)} %reshape.104), calls=%async_computation.6 | async-start | bytes 983040 | tf_op jit(solution)/shard_map/all_to_all | solution.py:127
  315.7 17.0 %reduce.3 = bf16[3072,80]{1,0:T(8,128)(2,1)S(1)} reduce(bf16[3072,1,1,80]{3,2,1,0:T(2,128)(2,1)S(1)} %reshape.100, bf16[]{:T(256)} %broadcast.25), dimensions={1,2}, to_apply=%reshape.100.reduce_sub_computation | reduce | bytes 983042 | tf_op jit(solution)/shard_map/broadcast_in_dim;stack;reshape | solution.py:122
  332.7 2.2 reshape.102
  334.9 7.3 %all-to-all-start.5 = ((bf16[16,2,7680]{2,1,0:T(2,128)(2,1)}), bf16[16,2,7680]{2,1,0:T(2,128)(2,1)S(1)}, u32[]{:S(2)}, u32[]{:S(2)}) async-start(bf16[16,2,7680]{2,1,0:T(2,128)(2,1)} %reshape.102), calls=%async_computation.5 | async-start | bytes 983040 | tf_op jit(solution)/shard_map/all_to_all | solution.py:126
  358.1 4.0 %reduce_sum.31 = f32[80,1280]{1,0:T(8,128)} reduce(f32[16,80,1280]{2,1,0:T(8,128)} %all-gather.5.cloned.1.call-done, f32[]{:T(128)} %constant.13.clone.1), dimensions={0}, to_apply=%region_7.8 | reduce | flops 1536000 | bytes 6963204 | tf_op jit(solution)/shard_map/reduce_sum | solution.py:33
  (115 shorter events, 62.8 us)
Async XLA Ops:
  8.0 1.0 copy-start
  8.0 101.7 %reduce-scatter.3.cloned.1.call-start = ((), (), s32[]{:S(2)}) async-start(), calls=%async_computation.11 | async-start | bytes 7372800 | tf_op jit(solution)/shard_map/reduce_scatter | solution.py:17
  14.3 1.0 copy-start.7
  14.3 95.4 %copy-start.8 = (bf16[1,192,1280]{2,1,0:T(8,128)(2,1)S(1)}, bf16[1,192,1280]{2,1,0:T(8,128)(2,1)}, u32[]{:S(2)}) copy-start(bf16[1,192,1280]{2,1,0:T(8,128)(2,1)} %param.8) | copy-start | bytes 1474564
  14.3 104.1 %copy-start.4 = (bf16[1,192,1280]{2,1,0:T(8,128)(2,1)S(1)}, bf16[1,192,1280]{2,1,0:T(8,128)(2,1)}, u32[]{:S(2)}) copy-start(bf16[1,192,1280]{2,1,0:T(8,128)(2,1)} %param.11) | copy-start | bytes 1474564
  14.4 105.1 %copy-start.9 = (bf16[1,192,1280]{2,1,0:T(8,128)(2,1)S(1)}, bf16[1,192,1280]{2,1,0:T(8,128)(2,1)}, u32[]{:S(2)}) copy-start(bf16[1,192,1280]{2,1,0:T(8,128)(2,1)} %param.9) | copy-start | bytes 1474564
  14.4 129.7 %all-gather.3.cloned.1.call-start = ((), (), s32[]{:S(2)}) async-start(), calls=%async_computation.10 | async-start | bytes 3481600 | tf_op jit(solution)/shard_map/all_gather | solution.py:94
  16.5 94.4 %all-to-all-start.3 = ((bf16[192,16,1,80]{0,3,2,1:T(8,128)(2,1)}), bf16[192,16,1,80]{0,3,2,1:T(8,128)(2,1)S(1)}, u32[]{:S(2)}, u32[]{:S(2)}) async-start(bf16[192,16,1,80]{0,3,2,1:T(8,128)(2,1)} %bitcast.17), calls=%async_computation.3 | async-start | bytes 1310720 | tf_op jit(solution)/shard_map/all_to_all | solution.py:109
  24.9 163.4 %reduce-scatter.5.cloned.1.call-start = ((), (), s32[]{:S(2)}) async-start(), calls=%async_computation.12 | async-start | bytes 1228800 | tf_op jit(solution)/shard_map/reduce_scatter | solution.py:17
  110.8 28.5 %all-to-all-start = ((bf16[192,16,1,80]{0,3,2,1:T(8,128)(2,1)}), bf16[192,16,1,80]{0,3,2,1:T(8,128)(2,1)S(1)}, u32[]{:S(2)}, u32[]{:S(2)}) async-start(bf16[192,16,1,80]{0,3,2,1:T(8,128)(2,1)} %bitcast.1), calls=%async_computation | async-start | bytes 1310720 | tf_op jit(solution)/shard_map/all_to_all | solution.py:107
  139.3 33.5 %copy-start.5 = (bf16[192,16,1,80]{0,3,2,1:T(8,128)(2,1)}, bf16[192,16,1,80]{0,3,2,1:T(8,128)(2,1)S(1)}, u32[]{:S(2)}) copy-start(bf16[192,16,1,80]{0,3,2,1:T(8,128)(2,1)S(1)} %all-to-all-done) | copy-start | bytes 1474564
  139.3 17.7 %all-to-all-start.1 = ((bf16[192,16,1,80]{0,3,2,1:T(8,128)(2,1)}), bf16[192,16,1,80]{0,3,2,1:T(8,128)(2,1)S(1)}, u32[]{:S(2)}, u32[]{:S(2)}) async-start(bf16[192,16,1,80]{0,3,2,1:T(8,128)(2,1)} %bitcast.124), calls=%async_computation.1 | async-start | bytes 1310720 | tf_op jit(solution)/shard_map/all_to_all | solution.py:108
  157.0 16.1 %copy-start.6 = (bf16[192,16,1,80]{0,3,2,1:T(8,128)(2,1)}, bf16[192,16,1,80]{0,3,2,1:T(8,128)(2,1)S(1)}, u32[]{:S(2)}) copy-start(bf16[192,16,1,80]{0,3,2,1:T(8,128)(2,1)S(1)} %all-to-all-done.1) | copy-start | bytes 1474564
  168.4 17.6 %all-to-all-start.2 = ((bf16[192,16,1,80]{0,3,2,1:T(8,128)(2,1)}), bf16[192,16,1,80]{0,3,2,1:T(8,128)(2,1)}, u32[]{:S(2)}, u32[]{:S(2)}) async-start(bf16[192,16,1,80]{0,3,2,1:T(8,128)(2,1)} %bitcast.12), calls=%async_computation.2 | async-start | bytes 1310720 | tf_op jit(solution)/shard_map/all_to_all | solution.py:110
  172.8 185.3 %all-gather.5.cloned.1.call-start = ((), (), s32[]{:S(2)}) async-start(), calls=%async_computation.13 | async-start | bytes 6963200 | tf_op jit(solution)/shard_map/all_gather | solution.py:32
  190.3 2.6 copy-start.2
  194.1 4.9 %copy-start.3 = (f32[512,3072]{1,0:T(8,128)S(1)}, f32[512,3072]{1,0:T(8,128)}, u32[]{:S(2)}) copy-start(f32[512,3072]{1,0:T(8,128)} %copy-done.2) | copy-start | bytes 18874372 | tf_op jit(solution)/shard_map/while
  207.3 2.6 copy-start.2
  211.1 4.6 %copy-start.3 = (f32[512,3072]{1,0:T(8,128)S(1)}, f32[512,3072]{1,0:T(8,128)}, u32[]{:S(2)}) copy-start(f32[512,3072]{1,0:T(8,128)} %copy-done.2) | copy-start | bytes 18874372 | tf_op jit(solution)/shard_map/while
  224.2 2.6 copy-start.2
  228.0 4.7 %copy-start.3 = (f32[512,3072]{1,0:T(8,128)S(1)}, f32[512,3072]{1,0:T(8,128)}, u32[]{:S(2)}) copy-start(f32[512,3072]{1,0:T(8,128)} %copy-done.2) | copy-start | bytes 18874372 | tf_op jit(solution)/shard_map/while
  241.2 2.6 copy-start.2
  244.9 5.0 %copy-start.3 = (f32[512,3072]{1,0:T(8,128)S(1)}, f32[512,3072]{1,0:T(8,128)}, u32[]{:S(2)}) copy-start(f32[512,3072]{1,0:T(8,128)} %copy-done.2) | copy-start | bytes 18874372 | tf_op jit(solution)/shard_map/while
  258.3 2.6 copy-start.2
  262.1 4.6 %copy-start.3 = (f32[512,3072]{1,0:T(8,128)S(1)}, f32[512,3072]{1,0:T(8,128)}, u32[]{:S(2)}) copy-start(f32[512,3072]{1,0:T(8,128)} %copy-done.2) | copy-start | bytes 18874372 | tf_op jit(solution)/shard_map/while
  275.2 2.6 copy-start.2
  279.0 4.6 %copy-start.3 = (f32[512,3072]{1,0:T(8,128)S(1)}, f32[512,3072]{1,0:T(8,128)}, u32[]{:S(2)}) copy-start(f32[512,3072]{1,0:T(8,128)} %copy-done.2) | copy-start | bytes 18874372 | tf_op jit(solution)/shard_map/while
  294.3 15.2 %all-to-all-start.7 = ((bf16[16,2,7680]{2,1,0:T(2,128)(2,1)}), bf16[16,2,7680]{2,1,0:T(2,128)(2,1)S(1)}, u32[]{:S(2)}, u32[]{:S(2)}) async-start(bf16[16,2,7680]{2,1,0:T(2,128)(2,1)} %reshape.106), calls=%async_computation.7 | async-start | bytes 983040 | tf_op jit(solution)/shard_map/all_to_all | solution.py:128
  309.5 25.4 %all-to-all-start.6 = ((bf16[16,2,7680]{2,1,0:T(2,128)(2,1)}), bf16[16,2,7680]{2,1,0:T(2,128)(2,1)S(1)}, u32[]{:S(2)}, u32[]{:S(2)}) async-start(bf16[16,2,7680]{2,1,0:T(2,128)(2,1)} %reshape.104), calls=%async_computation.6 | async-start | bytes 983040 | tf_op jit(solution)/shard_map/all_to_all | solution.py:127
  334.9 18.1 %all-to-all-start.5 = ((bf16[16,2,7680]{2,1,0:T(2,128)(2,1)}), bf16[16,2,7680]{2,1,0:T(2,128)(2,1)S(1)}, u32[]{:S(2)}, u32[]{:S(2)}) async-start(bf16[16,2,7680]{2,1,0:T(2,128)(2,1)} %reshape.102), calls=%async_computation.5 | async-start | bytes 983040 | tf_op jit(solution)/shard_map/all_to_all | solution.py:126
  353.0 9.0 %copy-start.1 = (bf16[1,192,1280]{2,1,0:T(8,128)(2,1)S(1)}, bf16[1,192,1280]{2,1,0:T(8,128)(2,1)}, u32[]{:S(2)}) copy-start(bf16[1,192,1280]{2,1,0:T(8,128)(2,1)} %param.12) | copy-start | bytes 1474564
Sparse Core Ops, SparseCore 0:
  14.5 95.1 reduce-scatter.2
  112.2 40.2 reduce-scatter.4
  188.4 64.1 all-gather.4
Sparse Core Ops, SparseCore 1:
  16.6 123.8 all-gather.2
where the time goes:
time: 371 us; the launch traced here: 369 us
  waiting for transfers between devices  127 us (34%)
  matrix products  81.9 us (22%)
  local copies, waits for them, and re-layouts  60.2 us (16%)
  starting transfers between devices  41.3 us (11%)
  other arithmetic  31.5 us (8%)
  between operations  15.4 us (4%)
  blocking collectives  11.4 us (3%)
    reduce_scatter x2, waiting for transfers between devices, reduced_to_own(): blocks = lax.psum_scatter(blocks, axes[k], scatter_dimension=0, tiled=True)  84.7 us
    unnamed x35, local copies, waits for them, and re-layouts  28.3 us
    dot_general x6, matrix products, one_block(): lax.dot_general(probs_low, dout_block, contract_first, preferred_element_...  26.2 us
    all_to_all x1, waiting for transfers between devices, body(): lax.all_to_all(split_heads(query), 'seq', split_axis=1, concat_axis=0, ti...  18.7 us
    dot_general x6, matrix products, one_block(): lax.dot_general(dout_block, values_h, contract_last, preferred_element_ty...  17.9 us
    while x24, local copies, waits for them, and re-layouts  17.7 us
    another operation x1, other arithmetic, body(): query_heads = jnp.stack(query_list, axis=1)[:, None]  17 us
    dot_general x6, matrix products, one_block(): lax.dot_general(query_block, keys_h, contract_last, preferred_element_typ...  11.8 us
  transfers between devices with their start and end apart: 11, of which 6 were waited for; matrix products, arithmetic and copies ran while one was open for 39% of the time, Pallas kernels for 0%

commit v1 on v0

--- a/solution.py
+++ b/solution.py
@@ -123,7 +123,15 @@
     keys_heads = jnp.stack(keys_list, axis=1)[:, None]
     values_heads = jnp.stack(values_list, axis=1)[:, None]
     query_back, keys_back, values_back = (
-        lax.all_to_all(query_heads, "seq", split_axis=0, concat_axis=1, tiled=True),
+        jnp.concatenate(
+            lax.all_to_all(
+                jnp.stack(jnp.split(query_heads, lax.psum(1, axis_name="seq"), axis=0)),
+                axis_name="seq",
+                split_axis=0,
+                concat_axis=0,
+            ),
+            axis=1,
+        ),
         lax.all_to_all(keys_heads, "seq", split_axis=0, concat_axis=1, tiled=True),
         lax.all_to_all(values_heads, "seq", split_axis=0, concat_axis=1, tiled=True),
     )

time: 371 us -> 374 us (level)
  local copies, waits for them, and re-layouts: 60.2 us -> 74.8 us
  other arithmetic: 31.5 us -> 17.5 us
  waiting for transfers between devices: 127 us -> 134 us
    another operation x1 -> x0, other arithmetic: 17 us -> none  [body(): query_heads = jnp.stack(query_list, axis=1)[:, None]]
    unnamed x35 -> x48, local copies, waits for them, and re-layouts: 28.3 us -> 41.8 us
    all_to_all x1, waiting for transfers between devices: 0.01 us -> 6.55 us  [body(): lax.all_to_all(keys_heads, 'seq', split_axis=0, concat_axis=1, tiled=True)]
    all_to_all x1, waiting for transfers between devices: 0.59 us -> 6.88 us  [body(): lax.all_to_all(jnp.stack(jnp.split(query_heads, lax.psum(1, axis_name='se...]
    all_to_all x1, waiting for transfers between devices: 7.58 us -> 1.45 us  [body(): lax.all_to_all(values_heads, 'seq', split_axis=0, concat_axis=1, tiled=True)]
    while x24 -> x37, local copies, waits for them, and re-layouts: 17.7 us -> 20.8 us
  transfers between devices with their start and end apart: 11 -> 11, of which waited for: 6 -> 7; matrix products, arithmetic and copies ran while one was open for 39% -> 38% of each run, Pallas kernels for 0% -> 0%
where the time goes in v1:
time: 374 us; the launch traced here: 372 us
  waiting for transfers between devices  134 us (36%)
  matrix products  80 us (21%)
  local copies, waits for them, and re-layouts  74.8 us (20%)
  starting transfers between devices  39 us (10%)
  other arithmetic  17.5 us (5%)
  between operations  15.4 us (4%)
  blocking collectives  11.4 us (3%)
    reduce_scatter x2, waiting for transfers between devices, reduced_to_own(): blocks = lax.psum_scatter(blocks, axes[k], scatter_dimension=0, tiled=True)  84.7 us
    unnamed x48, local copies, waits for them, and re-layouts  41.8 us
    dot_general x6, matrix products, one_block(): lax.dot_general(probs_low, dout_block, contract_first, preferred_element_...  26.2 us
    all_to_all x1, waiting for transfers between devices, body(): lax.all_to_all(split_heads(query), 'seq', split_axis=1, concat_axis=0, ti...  18.7 us
    while x36, local copies, waits for them, and re-layouts  18.6 us
    dot_general x6, matrix products, one_block(): lax.dot_general(dout_block, values_h, contract_last, preferred_element_ty...  16.1 us
    dot_general x6, matrix products, one_block(): lax.dot_general(query_block, keys_h, contract_last, preferred_element_typ...  11.8 us
    all_to_all x1, blocking collectives, body(): lax.all_to_all(row_local, 'seq', split_axis=1, concat_axis=0, tiled=True)  11.4 us
  transfers between devices with their start and end apart: 11, of which 7 were waited for; matrix products, arithmetic and copies ran while one was open for 38% of the time, Pallas kernels for 0%

profile of v1, /device:TPU:1, one launch (start us, length us, event | category | flops | bytes accessed | tf_op | source)
XLA Modules:
  0.0 372.2 jit_solution(3194361169450053772)
XLA Ops:
  9.0 2.1 convolution_multiply_fusion
  11.1 3.2 copy.113
  16.4 8.4 %all-to-all-start.3 = ((bf16[192,16,1,80]{0,3,2,1:T(8,128)(2,1)}), bf16[192,16,1,80]{0,3,2,1:T(8,128)(2,1)S(1)}, u32[]{:S(2)}, u32[]{:S(2)}) async-start(bf16[192,16,1,80]{0,3,2,1:T(8,128)(2,1)} %bitcast.17), calls=%async_computation.3 | async-start | bytes 1310720 | tf_op jit(solution)/shard_map/all_to_all | solution.py:109
  24.9 84.7 %reduce-scatter.3.cloned.1.call-done = f32[2,80,1280]{2,1,0:T(8,128)} async-done(((f32[16,80,1280]{2,1,0:T(8,128)}), f32[2,80,1280]{2,1,0:T(8,128)}) %reduce-scatter.3.cloned.1.call-update) | async-done | bytes 819216 | tf_op jit(solution)/shard_map/reduce_scatter | solution.py:17
  110.8 7.6 %all-to-all-start = ((bf16[192,16,1,80]{0,3,2,1:T(8,128)(2,1)}), bf16[192,16,1,80]{0,3,2,1:T(8,128)(2,1)S(1)}, u32[]{:S(2)}, u32[]{:S(2)}) async-start(bf16[192,16,1,80]{0,3,2,1:T(8,128)(2,1)} %bitcast.1), calls=%async_computation | async-start | bytes 1310720 | tf_op jit(solution)/shard_map/all_to_all | solution.py:107
  120.5 18.7 %all-to-all-done = bf16[192,16,1,80]{0,3,2,1:T(8,128)(2,1)S(1)} async-done(((bf16[192,16,1,80]{0,3,2,1:T(8,128)(2,1)}), bf16[192,16,1,80]{0,3,2,1:T(8,128)(2,1)S(1)}, u32[]{:S(2)}, u32[]{:S(2)}) %all-to-all-start) | async-done | bytes 491552 | tf_op jit(solution)/shard_map/all_to_all | solution.py:107
  139.3 4.9 %all-to-all-start.1 = ((bf16[192,16,1,80]{0,3,2,1:T(8,128)(2,1)}), bf16[192,16,1,80]{0,3,2,1:T(8,128)(2,1)S(1)}, u32[]{:S(2)}, u32[]{:S(2)}) async-start(bf16[192,16,1,80]{0,3,2,1:T(8,128)(2,1)} %bitcast.188), calls=%async_computation.1 | async-start | bytes 1310720 | tf_op jit(solution)/shard_map/all_to_all | solution.py:108
  144.1 3.2 convolution_convert_fusion.1
  149.9 7.1 %all-to-all-done.1 = bf16[192,16,1,80]{0,3,2,1:T(8,128)(2,1)S(1)} async-done(((bf16[192,16,1,80]{0,3,2,1:T(8,128)(2,1)}), bf16[192,16,1,80]{0,3,2,1:T(8,128)(2,1)S(1)}, u32[]{:S(2)}, u32[]{:S(2)}) %all-to-all-start.1) | async-done | bytes 491552 | tf_op jit(solution)/shard_map/all_to_all | solution.py:108
  157.0 11.4 %all_to_all.110 = f32[192,16,1]{0,2,1:T(1,128)S(1)} all-to-all(f32[192,16,1]{0,2,1:T(1,128)S(1)} %reduce_sum.30), channel_id=1, replica_groups=mesh['seq'=16,'dp_0'=2,'dp_1'=8] {'seq'}, dimensions={1} | all-to-all | bytes 24576 | tf_op jit(solution)/shard_map/all_to_all | solution.py:105
  168.4 4.4 %all-to-all-start.2 = ((bf16[192,16,1,80]{0,3,2,1:T(8,128)(2,1)}), bf16[192,16,1,80]{0,3,2,1:T(8,128)(2,1)}, u32[]{:S(2)}, u32[]{:S(2)}) async-start(bf16[192,16,1,80]{0,3,2,1:T(8,128)(2,1)} %bitcast.12), calls=%async_computation.2 | async-start | bytes 1310720 | tf_op jit(solution)/shard_map/all_to_all | solution.py:110
  174.3 2.4 copy.117
  178.2 7.7 %all-to-all-done.2 = bf16[192,16,1,80]{0,3,2,1:T(8,128)(2,1)} async-done(((bf16[192,16,1,80]{0,3,2,1:T(8,128)(2,1)}), bf16[192,16,1,80]{0,3,2,1:T(8,128)(2,1)}, u32[]{:S(2)}, u32[]{:S(2)}) %all-to-all-start.2) | async-done | bytes 491552 | tf_op jit(solution)/shard_map/all_to_all | solution.py:110
  186.0 2.3 copy.119
  188.3 100.8 %while.15 = (s32[]{:T(128)}, f32[3072,80]{0,1:T(8,128)S(1)}, f32[3072,80]{0,1:T(8,128)S(1)}, bf16[6,512,80]{1,2,0:T(8,128)(2,1)}, bf16[6,512,80]{2,1,0:T(8,128)(...) while((s32[]{:T(128)}, f32[3072,80]{0,1:T(8,128)S(1)}, ...), condition=%wide.region_4.5_spmd.clone, body=%wide.region_1.4_spmd.clone.sunk | while | flops 1281334784 | bytes 92938952 | solution.py:76
  188.3 2.0 multiply_reduce_fusion.2
  190.3 2.6 copy-done.1
  194.1 4.5 %convolution_add_fusion.5 = f32[3072,80]{0,1:T(8,128)S(1)} fusion(f32[512,3072]{1,0:T(8,128)} %copy-done.1, f32[512]{0:T(512)S(1)} %log_add_fusion.2, f32[3072,80]{0,1:T(8,128)S(1)} %get-tuple-element.223, pred[]{:T(512)S(6)} %compare.3, bf16[6,512,80]{2,1,0:T(8,128)(2,1)} %get-tuple-element.238, s32[]{:T(128)} %get-tuple-element.221), kind=kOutput, calls=%fused_computation.5.clone.1 | convolution fusion | flops 256868352 | bytes 8391169 | tf_op jit(solution)/shard_map/while/body/eval_jaxpr/dot_general | solution.py:57
  199.0 2.7 multiply_convert_fusion.2
  207.1 2.6 copy-done.1
  210.9 4.3 %convolution_add_fusion.5 = f32[3072,80]{0,1:T(8,128)S(1)} fusion(f32[512,3072]{1,0:T(8,128)} %copy-done.1, f32[512]{0:T(512)S(1)} %log_add_fusion.2, f32[3072,80]{0,1:T(8,128)S(1)} %get-tuple-element.223, pred[]{:T(512)S(6)} %compare.3, bf16[6,512,80]{2,1,0:T(8,128)(2,1)} %get-tuple-element.238, s32[]{:T(128)} %get-tuple-element.221), kind=kOutput, calls=%fused_computation.5.clone.1 | convolution fusion | flops 256868352 | bytes 8391169 | tf_op jit(solution)/shard_map/while/body/eval_jaxpr/dot_general | solution.py:57
  215.7 2.7 multiply_convert_fusion.2
  223.8 2.6 copy-done.1
  227.6 4.4 %convolution_add_fusion.5 = f32[3072,80]{0,1:T(8,128)S(1)} fusion(f32[512,3072]{1,0:T(8,128)} %copy-done.1, f32[512]{0:T(512)S(1)} %log_add_fusion.2, f32[3072,80]{0,1:T(8,128)S(1)} %get-tuple-element.223, pred[]{:T(512)S(6)} %compare.3, bf16[6,512,80]{2,1,0:T(8,128)(2,1)} %get-tuple-element.238, s32[]{:T(128)} %get-tuple-element.221), kind=kOutput, calls=%fused_computation.5.clone.1 | convolution fusion | flops 256868352 | bytes 8391169 | tf_op jit(solution)/shard_map/while/body/eval_jaxpr/dot_general | solution.py:57
  232.5 2.7 multiply_convert_fusion.2
  240.6 2.6 copy-done.1
  244.4 4.4 %convolution_add_fusion.5 = f32[3072,80]{0,1:T(8,128)S(1)} fusion(f32[512,3072]{1,0:T(8,128)} %copy-done.1, f32[512]{0:T(512)S(1)} %log_add_fusion.2, f32[3072,80]{0,1:T(8,128)S(1)} %get-tuple-element.223, pred[]{:T(512)S(6)} %compare.3, bf16[6,512,80]{2,1,0:T(8,128)(2,1)} %get-tuple-element.238, s32[]{:T(128)} %get-tuple-element.221), kind=kOutput, calls=%fused_computation.5.clone.1 | convolution fusion | flops 256868352 | bytes 8391169 | tf_op jit(solution)/shard_map/while/body/eval_jaxpr/dot_general | solution.py:57
  249.5 2.7 multiply_convert_fusion.2
  257.7 2.6 copy-done.1
  261.5 4.3 %convolution_add_fusion.5 = f32[3072,80]{0,1:T(8,128)S(1)} fusion(f32[512,3072]{1,0:T(8,128)} %copy-done.1, f32[512]{0:T(512)S(1)} %log_add_fusion.2, f32[3072,80]{0,1:T(8,128)S(1)} %get-tuple-element.223, pred[]{:T(512)S(6)} %compare.3, bf16[6,512,80]{2,1,0:T(8,128)(2,1)} %get-tuple-element.238, s32[]{:T(128)} %get-tuple-element.221), kind=kOutput, calls=%fused_computation.5.clone.1 | convolution fusion | flops 256868352 | bytes 8391169 | tf_op jit(solution)/shard_map/while/body/eval_jaxpr/dot_general | solution.py:57
  266.3 2.7 multiply_convert_fusion.2
  272.4 2.0 multiply_reduce_fusion.2
  274.4 2.6 copy-done.1
  278.2 4.3 %convolution_add_fusion.5 = f32[3072,80]{0,1:T(8,128)S(1)} fusion(f32[512,3072]{1,0:T(8,128)} %copy-done.1, f32[512]{0:T(512)S(1)} %log_add_fusion.2, f32[3072,80]{0,1:T(8,128)S(1)} %get-tuple-element.223, pred[]{:T(512)S(6)} %compare.3, bf16[6,512,80]{2,1,0:T(8,128)(2,1)} %get-tuple-element.238, s32[]{:T(128)} %get-tuple-element.221), kind=kOutput, calls=%fused_computation.5.clone.1 | convolution fusion | flops 256868352 | bytes 8391169 | tf_op jit(solution)/shard_map/while/body/eval_jaxpr/dot_general | solution.py:57
  283.0 2.7 multiply_convert_fusion.2
  289.1 2.2 copy.106
  303.5 4.1 %all-to-all-start.5 = ((bf16[16,192,1,1,80]{1,4,3,2,0:T(8,128)(2,1)}), bf16[16,192,1,1,80]{1,4,3,2,0:T(8,128)(2,1)S(1)}, u32[]{:S(2)}, u32[]{:S(2)}) async-start(bf16[16,192,1,1,80]{1,4,3,2,0:T(8,128)(2,1)} %fusion.24), calls=%async_computation.5 | async-start | bytes 1310720 | tf_op jit(solution)/shard_map/all_to_all | solution.py:127
  309.2 2.0 reduce.3
  311.5 2.2 reshape.100
  313.8 6.9 %all-to-all-done.5 = bf16[16,192,1,1,80]{1,4,3,2,0:T(8,128)(2,1)S(1)} async-done(((bf16[16,192,1,1,80]{1,4,3,2,0:T(8,128)(2,1)}), bf16[16,192,1,1,80]{1,4,3,2,0:T(8,128)(2,1)S(1)}, u32[]{:S(2)}, u32[]{:S(2)}) %all-to-all-start.5) | async-done | bytes 491552 | tf_op jit(solution)/shard_map/all_to_all | solution.py:127
  320.7 4.3 %all-to-all-start.6 = ((bf16[16,2,7680]{2,1,0:T(2,128)(2,1)}), bf16[16,2,7680]{2,1,0:T(2,128)(2,1)S(1)}, u32[]{:S(2)}, u32[]{:S(2)}) async-start(bf16[16,2,7680]{2,1,0:T(2,128)(2,1)} %reshape.100), calls=%async_computation.6 | async-start | bytes 983040 | tf_op jit(solution)/shard_map/all_to_all | solution.py:135
  324.9 2.0 reduce.4
  327.3 2.3 reshape.102
  329.5 6.5 %all-to-all-done.6 = bf16[16,2,7680]{2,1,0:T(2,128)(2,1)S(1)} async-done(((bf16[16,2,7680]{2,1,0:T(2,128)(2,1)}), bf16[16,2,7680]{2,1,0:T(2,128)(2,1)S(1)}, u32[]{:S(2)}, u32[]{:S(2)}) %all-to-all-start.6) | async-done | bytes 491552 | tf_op jit(solution)/shard_map/all_to_all | solution.py:135
  336.1 5.0 %all-to-all-start.7 = ((bf16[16,2,7680]{2,1,0:T(2,128)(2,1)}), bf16[16,2,7680]{2,1,0:T(2,128)(2,1)}, u32[]{:S(2)}, u32[]{:S(2)}) async-start(bf16[16,2,7680]{2,1,0:T(2,128)(2,1)} %reshape.102), calls=%async_computation.7 | async-start | bytes 983040 | tf_op jit(solution)/shard_map/all_to_all | solution.py:136
  342.1 5.3 %reshape.101 = bf16[3072,1,1,80]{3,2,1,0:T(2,128)(2,1)S(1)} reshape(bf16[16,2,7680]{2,1,0:T(2,128)(2,1)} %copy-done.7) | data formatting | bytes 983040
  352.3 5.3 %reshape.103 = bf16[3072,1,1,80]{3,2,1,0:T(2,128)(2,1)S(1)} reshape(bf16[16,2,7680]{2,1,0:T(2,128)(2,1)} %all-to-all-done.7) | data formatting | bytes 983040
  361.1 4.0 %reduce_sum.31 = f32[80,1280]{1,0:T(8,128)} reduce(f32[16,80,1280]{2,1,0:T(8,128)} %all-gather.5.cloned.1.call-done, f32[]{:T(128)} %constant.13.clone.1), dimensions={0}, to_apply=%region_7.8 | reduce | flops 1536000 | bytes 6963204 | tf_op jit(solution)/shard_map/reduce_sum | solution.py:33
  (137 shorter events, 74.7 us)
Async XLA Ops:
  8.0 1.0 copy-start
  8.0 101.6 %reduce-scatter.3.cloned.1.call-start = ((), (), s32[]{:S(2)}) async-start(), calls=%async_computation.11 | async-start | bytes 7372800 | tf_op jit(solution)/shard_map/reduce_scatter | solution.py:17
  14.3 1.0 copy-start.8
  14.3 95.3 %copy-start.9 = (bf16[1,192,1280]{2,1,0:T(8,128)(2,1)S(1)}, bf16[1,192,1280]{2,1,0:T(8,128)(2,1)}, u32[]{:S(2)}) copy-start(bf16[1,192,1280]{2,1,0:T(8,128)(2,1)} %param.8) | copy-start | bytes 1474564
  14.3 104.0 %copy-start.4 = (bf16[1,192,1280]{2,1,0:T(8,128)(2,1)S(1)}, bf16[1,192,1280]{2,1,0:T(8,128)(2,1)}, u32[]{:S(2)}) copy-start(bf16[1,192,1280]{2,1,0:T(8,128)(2,1)} %param.11) | copy-start | bytes 1474564
  14.3 105.1 %copy-start.10 = (bf16[1,192,1280]{2,1,0:T(8,128)(2,1)S(1)}, bf16[1,192,1280]{2,1,0:T(8,128)(2,1)}, u32[]{:S(2)}) copy-start(bf16[1,192,1280]{2,1,0:T(8,128)(2,1)} %param.9) | copy-start | bytes 1474564
  14.4 129.8 %all-gather.3.cloned.1.call-start = ((), (), s32[]{:S(2)}) async-start(), calls=%async_computation.10 | async-start | bytes 3481600 | tf_op jit(solution)/shard_map/all_gather | solution.py:94
  16.4 94.3 %all-to-all-start.3 = ((bf16[192,16,1,80]{0,3,2,1:T(8,128)(2,1)}), bf16[192,16,1,80]{0,3,2,1:T(8,128)(2,1)S(1)}, u32[]{:S(2)}, u32[]{:S(2)}) async-start(bf16[192,16,1,80]{0,3,2,1:T(8,128)(2,1)} %bitcast.17), calls=%async_computation.3 | async-start | bytes 1310720 | tf_op jit(solution)/shard_map/all_to_all | solution.py:109
  24.9 163.3 %reduce-scatter.5.cloned.1.call-start = ((), (), s32[]{:S(2)}) async-start(), calls=%async_computation.12 | async-start | bytes 1228800 | tf_op jit(solution)/shard_map/reduce_scatter | solution.py:17
  110.8 28.5 %all-to-all-start = ((bf16[192,16,1,80]{0,3,2,1:T(8,128)(2,1)}), bf16[192,16,1,80]{0,3,2,1:T(8,128)(2,1)S(1)}, u32[]{:S(2)}, u32[]{:S(2)}) async-start(bf16[192,16,1,80]{0,3,2,1:T(8,128)(2,1)} %bitcast.1), calls=%async_computation | async-start | bytes 1310720 | tf_op jit(solution)/shard_map/all_to_all | solution.py:107
  139.3 33.5 %copy-start.5 = (bf16[192,16,1,80]{0,3,2,1:T(8,128)(2,1)}, bf16[192,16,1,80]{0,3,2,1:T(8,128)(2,1)S(1)}, u32[]{:S(2)}) copy-start(bf16[192,16,1,80]{0,3,2,1:T(8,128)(2,1)S(1)} %all-to-all-done) | copy-start | bytes 1474564
  139.3 17.8 %all-to-all-start.1 = ((bf16[192,16,1,80]{0,3,2,1:T(8,128)(2,1)}), bf16[192,16,1,80]{0,3,2,1:T(8,128)(2,1)S(1)}, u32[]{:S(2)}, u32[]{:S(2)}) async-start(bf16[192,16,1,80]{0,3,2,1:T(8,128)(2,1)} %bitcast.188), calls=%async_computation.1 | async-start | bytes 1310720 | tf_op jit(solution)/shard_map/all_to_all | solution.py:108
  157.0 16.0 %copy-start.6 = (bf16[192,16,1,80]{0,3,2,1:T(8,128)(2,1)}, bf16[192,16,1,80]{0,3,2,1:T(8,128)(2,1)S(1)}, u32[]{:S(2)}) copy-start(bf16[192,16,1,80]{0,3,2,1:T(8,128)(2,1)S(1)} %all-to-all-done.1) | copy-start | bytes 1474564
  168.4 17.5 %all-to-all-start.2 = ((bf16[192,16,1,80]{0,3,2,1:T(8,128)(2,1)}), bf16[192,16,1,80]{0,3,2,1:T(8,128)(2,1)}, u32[]{:S(2)}, u32[]{:S(2)}) async-start(bf16[192,16,1,80]{0,3,2,1:T(8,128)(2,1)} %bitcast.12), calls=%async_computation.2 | async-start | bytes 1310720 | tf_op jit(solution)/shard_map/all_to_all | solution.py:110
  172.8 188.3 %all-gather.5.cloned.1.call-start = ((), (), s32[]{:S(2)}) async-start(), calls=%async_computation.13 | async-start | bytes 6963200 | tf_op jit(solution)/shard_map/all_gather | solution.py:32
  190.2 2.6 copy-start.1
  194.0 4.8 %copy-start.2 = (f32[512,3072]{1,0:T(8,128)S(1)}, f32[512,3072]{1,0:T(8,128)}, u32[]{:S(2)}) copy-start(f32[512,3072]{1,0:T(8,128)} %copy-done.1) | copy-start | bytes 18874372 | tf_op jit(solution)/shard_map/while
  194.0 5.0 %copy-start.3 = (bf16[3072,80]{1,0:T(8,128)(2,1)S(1)}, bf16[3072,80]{1,0:T(8,128)(2,1)}, u32[]{:S(2)}) copy-start(bf16[3072,80]{1,0:T(8,128)(2,1)} %get-tuple-element.239) | copy-start | bytes 1474564 | tf_op jit(solution)/shard_map/while
  207.1 2.6 copy-start.1
  210.9 4.6 %copy-start.2 = (f32[512,3072]{1,0:T(8,128)S(1)}, f32[512,3072]{1,0:T(8,128)}, u32[]{:S(2)}) copy-start(f32[512,3072]{1,0:T(8,128)} %copy-done.1) | copy-start | bytes 18874372 | tf_op jit(solution)/shard_map/while
  210.9 4.8 %copy-start.3 = (bf16[3072,80]{1,0:T(8,128)(2,1)S(1)}, bf16[3072,80]{1,0:T(8,128)(2,1)}, u32[]{:S(2)}) copy-start(bf16[3072,80]{1,0:T(8,128)(2,1)} %get-tuple-element.239) | copy-start | bytes 1474564 | tf_op jit(solution)/shard_map/while
  223.8 2.6 copy-start.1
  227.6 4.7 %copy-start.2 = (f32[512,3072]{1,0:T(8,128)S(1)}, f32[512,3072]{1,0:T(8,128)}, u32[]{:S(2)}) copy-start(f32[512,3072]{1,0:T(8,128)} %copy-done.1) | copy-start | bytes 18874372 | tf_op jit(solution)/shard_map/while
  227.6 4.9 %copy-start.3 = (bf16[3072,80]{1,0:T(8,128)(2,1)S(1)}, bf16[3072,80]{1,0:T(8,128)(2,1)}, u32[]{:S(2)}) copy-start(bf16[3072,80]{1,0:T(8,128)(2,1)} %get-tuple-element.239) | copy-start | bytes 1474564 | tf_op jit(solution)/shard_map/while
  240.6 2.6 copy-start.1
  244.4 4.9 %copy-start.2 = (f32[512,3072]{1,0:T(8,128)S(1)}, f32[512,3072]{1,0:T(8,128)}, u32[]{:S(2)}) copy-start(f32[512,3072]{1,0:T(8,128)} %copy-done.1) | copy-start | bytes 18874372 | tf_op jit(solution)/shard_map/while
  244.4 5.1 %copy-start.3 = (bf16[3072,80]{1,0:T(8,128)(2,1)S(1)}, bf16[3072,80]{1,0:T(8,128)(2,1)}, u32[]{:S(2)}) copy-start(bf16[3072,80]{1,0:T(8,128)(2,1)} %get-tuple-element.239) | copy-start | bytes 1474564 | tf_op jit(solution)/shard_map/while
  257.7 2.6 copy-start.1
  261.5 4.6 %copy-start.2 = (f32[512,3072]{1,0:T(8,128)S(1)}, f32[512,3072]{1,0:T(8,128)}, u32[]{:S(2)}) copy-start(f32[512,3072]{1,0:T(8,128)} %copy-done.1) | copy-start | bytes 18874372 | tf_op jit(solution)/shard_map/while
  261.5 4.8 %copy-start.3 = (bf16[3072,80]{1,0:T(8,128)(2,1)S(1)}, bf16[3072,80]{1,0:T(8,128)(2,1)}, u32[]{:S(2)}) copy-start(bf16[3072,80]{1,0:T(8,128)(2,1)} %get-tuple-element.239) | copy-start | bytes 1474564 | tf_op jit(solution)/shard_map/while
  274.4 2.6 copy-start.1
  278.2 4.6 %copy-start.2 = (f32[512,3072]{1,0:T(8,128)S(1)}, f32[512,3072]{1,0:T(8,128)}, u32[]{:S(2)}) copy-start(f32[512,3072]{1,0:T(8,128)} %copy-done.1) | copy-start | bytes 18874372 | tf_op jit(solution)/shard_map/while
  278.2 4.8 %copy-start.3 = (bf16[3072,80]{1,0:T(8,128)(2,1)S(1)}, bf16[3072,80]{1,0:T(8,128)(2,1)}, u32[]{:S(2)}) copy-start(bf16[3072,80]{1,0:T(8,128)(2,1)} %get-tuple-element.239) | copy-start | bytes 1474564 | tf_op jit(solution)/shard_map/while
  303.5 17.2 %all-to-all-start.5 = ((bf16[16,192,1,1,80]{1,4,3,2,0:T(8,128)(2,1)}), bf16[16,192,1,1,80]{1,4,3,2,0:T(8,128)(2,1)S(1)}, u32[]{:S(2)}, u32[]{:S(2)}) async-start(bf16[16,192,1,1,80]{1,4,3,2,0:T(8,128)(2,1)} %fusion.24), calls=%async_computation.5 | async-start | bytes 1310720 | tf_op jit(solution)/shard_map/all_to_all | solution.py:127
  320.7 15.4 %all-to-all-start.6 = ((bf16[16,2,7680]{2,1,0:T(2,128)(2,1)}), bf16[16,2,7680]{2,1,0:T(2,128)(2,1)S(1)}, u32[]{:S(2)}, u32[]{:S(2)}) async-start(bf16[16,2,7680]{2,1,0:T(2,128)(2,1)} %reshape.100), calls=%async_computation.6 | async-start | bytes 983040 | tf_op jit(solution)/shard_map/all_to_all | solution.py:135
  336.1 5.0 %copy-start.7 = (bf16[16,2,7680]{2,1,0:T(2,128)(2,1)}, bf16[16,2,7680]{2,1,0:T(2,128)(2,1)S(1)}, u32[]{:S(2)}) copy-start(bf16[16,2,7680]{2,1,0:T(2,128)(2,1)S(1)} %all-to-all-done.6) | copy-start | bytes 1474564
  336.1 16.3 %all-to-all-start.7 = ((bf16[16,2,7680]{2,1,0:T(2,128)(2,1)}), bf16[16,2,7680]{2,1,0:T(2,128)(2,1)}, u32[]{:S(2)}, u32[]{:S(2)}) async-start(bf16[16,2,7680]{2,1,0:T(2,128)(2,1)} %reshape.102), calls=%async_computation.7 | async-start | bytes 983040 | tf_op jit(solution)/shard_map/all_to_all | solution.py:136
Sparse Core Ops, SparseCore 0:
  14.5 95.1 reduce-scatter.2
  112.2 40.2 reduce-scatter.4
  188.4 64.0 all-gather.4
Sparse Core Ops, SparseCore 1:
  16.6 123.6 all-gather.2
